TPU v7x, 32 devices: a whole 2x2x4 slice. The times are simulated.
32 devices in a mesh: dp: 8 (over y, x, core), tensor: 4 (over z).
Axes of the slice: x: 2, y: 2, z: 4, core: 2. Of those that a mesh axis runs over, the one named last changes fastest.
Arguments:
- enc_hidden: bfloat16 [16384, 4096], P(('dp', 'tensor')), parts along dimension 0, may hold values from -6 to 6
- enc_gain: float32 [4096], replicated, may hold values from 0.1 to 1.9
- dec_hidden: bfloat16 [4096, 4096], P(('dp', 'tensor')), parts along dimension 0, may hold values from -6 to 6
- dec_gain: float32 [4096], replicated, may hold values from 0.8 to 12, as said below
- w_query: bfloat16 [4096, 4096], P(None, 'tensor'), may hold values from -0.046875 to 0.046875
- w_key: bfloat16 [4096, 4096], P(None, 'tensor'), may hold values from -0.09375 to 0.09375
- w_value: bfloat16 [4096, 4096], P(None, 'tensor'), may hold values from -0.09375 to 0.09375
- w_out: bfloat16 [4096, 4096], P('tensor'), may hold values from -0.75 to 0.75
- enc_length: int32 [8], P('dp'), parts along dimension 0, may hold values from 1024 to 2048
- dec_length: int32 [8], P('dp'), parts along dimension 0, may hold values from 256 to 512
Outputs:
- memory: bfloat16 [16384, 4096], P(('dp', 'tensor')), parts along dimension 0
- cross_out: bfloat16 [4096, 4096], P(('dp', 'tensor')), parts along dimension 0
There are 8 independent parts, one for each index of `dp`. A program takes and returns all parts, laid end to end along the dimension named above; an argument that names none is the same for every part. Nothing has to cross between parts.
Inputs may be any that keep to these rules, and one draw needn't show every extreme that they name: `dec_gain`: positive.
All inputs are finite; a program needn't handle non-finite values.
Results may differ from a plain program's by a relative error of at most 0.02.
The roundings to bfloat16 on the way count: a program that leaves them out, or rounds other values in their place, can miss the bound.
Values may be sent and summed in bfloat16 or wider, within the bound.
No kernel may reach another device: no remote copies, remote signals or barrier semaphores. Data moves between devices by JAX's collectives and lax.ppermute only.
A program may use at most 192 MiB of HBM per device.

v0:
```python
import jax
import jax.numpy as jnp
from jax import lax
from jax.sharding import PartitionSpec as P

HEAD_DIM = 64
ENC_LEN = 2048
DEC_LEN = 512


def rms_norm(values, gain):
    wide = values.astype(jnp.float32)
    mean_sq = jnp.mean(wide * wide, axis=-1, keepdims=True)
    return (wide * lax.rsqrt(mean_sq + 1e-06) * gain).astype(jnp.bfloat16)


def shards(
    enc_hidden,
    enc_gain,
    dec_hidden,
    dec_gain,
    w_query,
    w_key,
    w_value,
    w_out,
    enc_length,
    dec_length,
):
    memory = rms_norm(enc_hidden, enc_gain)
    normed = rms_norm(dec_hidden, dec_gain)
    local_width = w_query.shape[1]
    local_heads = local_width // HEAD_DIM
    dec_rows = dec_hidden.shape[0]
    all_normed = lax.all_gather(normed, "tensor", axis=0, tiled=True)
    queries = jnp.dot(all_normed, w_query, preferred_element_type=jnp.float32).astype(jnp.bfloat16)
    q_heads = queries.reshape(DEC_LEN, local_heads, HEAD_DIM)
    segment = lax.all_gather(memory, "tensor", axis=0, tiled=True)
    key_part = jnp.dot(segment, w_key, preferred_element_type=jnp.float32).astype(jnp.bfloat16)
    value_part = jnp.dot(segment, w_value, preferred_element_type=jnp.float32).astype(jnp.bfloat16)
    paired = jnp.concatenate([key_part, value_part], axis=1)
    key_rows = paired[:, :local_width]
    value_rows = paired[:, local_width:]
    k_heads = key_rows.reshape(ENC_LEN, local_heads, HEAD_DIM)
    scores = jnp.einsum("qhd,khd->hqk", q_heads, k_heads, preferred_element_type=jnp.float32)
    valid_keys = jnp.arange(ENC_LEN, dtype=jnp.int32) < enc_length[0]
    scores = jnp.where(valid_keys[None, None, :], scores, -jnp.inf)
    weights = jax.nn.softmax(scores, axis=-1).astype(jnp.bfloat16)
    v_heads = value_rows.reshape(ENC_LEN, local_heads, HEAD_DIM)
    context = jnp.einsum("hqk,khd->qhd", weights, v_heads, preferred_element_type=jnp.float32)
    context = context.astype(jnp.bfloat16).reshape(DEC_LEN, local_width)
    projected = lax.psum_scatter(
        jnp.dot(context, w_out, preferred_element_type=jnp.float32).astype(jnp.bfloat16),
        "tensor",
        scatter_dimension=0,
        tiled=True,
    ).astype(jnp.float32)
    row_ids = lax.axis_index("tensor") * dec_rows + jnp.arange(dec_rows, dtype=jnp.int32)
    live_rows = row_ids < dec_length[0]
    cross_out = jnp.where(live_rows[:, None], projected, 0.0).astype(jnp.bfloat16)
    return (memory, cross_out)


def solution(mesh):
    placed = (
        P(("dp", "tensor"), None),
        P(),
        P(("dp", "tensor"), None),
        P(),
        P(None, "tensor"),
        P(None, "tensor"),
        P(None, "tensor"),
        P("tensor", None),
        P("dp"),
        P("dp"),
    )
    return jax.shard_map(
        shards,
        mesh=mesh,
        in_specs=placed,
        out_specs=(P(("dp", "tensor"), None), P(("dp", "tensor"), None)),
        check_vma=False,
    )
```

profile of v0, /device:TPU:0, one launch (start us, length us, event | category | flops | bytes accessed | tf_op | source)
XLA Modules:
  0.0 576.0 jit_solution(13626997619669954659)
XLA Ops:
  7.2 0.0 copy-start
  7.2 0.0 all-gather.5.cloned.1.call-start
  7.2 1.5 fusion.10
  8.7 2.5 fusion.12
  11.3 0.0 all-gather.5.cloned.1.call-update
  11.3 0.0 all-gather.3.cloned.1.call-start
  11.4 3.1 fusion.7
  14.4 0.0 copy-done
  14.5 5.8 %fusion.9 = bf16[512,4096]{1,0:T(8,128)(2,1)} fusion(bf16[512,4096]{1,0:T(8,128)(2,1)} %param.10, f32[4096]{0:T(1024)S(1)} %copy-done, f32[512]{0:T(512)S(1)} %add_rsqrt_fusion), kind=kLoop, calls=%fused_computation.12 | loop fusion | flops 8388608 | bytes 8407040 | tf_op jit(solution)/shard_map/convert_element_type | solution.py:14
  20.3 0.0 all-gather.3.cloned.1.call-update
  20.3 0.0 reduce-scatter.2.cloned.1.call-start
  21.0 73.9 %all-gather.5.cloned.1.call-done = bf16[512,4096]{1,0:T(8,128)(2,1)} async-done(((bf16[128,4096]{1,0:T(8,128)(2,1)}), bf16[512,4096]{1,0:T(8,128)(2,1)}) %all-gather.5.cloned.1.call-update) | async-done | bytes 4194320 | tf_op jit(solution)/shard_map/all_gather | solution.py:34
  94.9 9.1 %convolution_convert_fusion.3 = bf16[512,1024]{1,0:T(8,128)(2,1)S(1)} fusion(bf16[512,4096]{1,0:T(8,128)(2,1)} %all-gather.5.cloned.1.call-done, bf16[4096,1024]{1,0:T(8,128)(2,1)} %param.14), kind=kOutput, calls=%fused_computation.22 | convolution fusion | flops 4295491584 | bytes 13631488 | tf_op jit(solution)/shard_map/dot_general | solution.py:35
  104.1 0.7 copy.13
  104.8 277.5 %all-gather.3.cloned.1.call-done = bf16[2048,4096]{1,0:T(8,128)(2,1)} async-done(((bf16[512,4096]{1,0:T(8,128)(2,1)}), bf16[2048,4096]{1,0:T(8,128)(2,1)}) %all-gather.3.cloned.1.call-update) | async-done | bytes 16777232 | tf_op jit(solution)/shard_map/all_gather | solution.py:37
  382.3 23.9 %convolution_convert_fusion.1 = bf16[2048,1024]{0,1:T(8,128)(2,1)} fusion(bf16[2048,4096]{1,0:T(8,128)(2,1)} %all-gather.3.cloned.1.call-done, bf16[4096,1024]{1,0:T(8,128)(2,1)} %param.15), kind=kOutput, calls=%fused_computation.14 | convolution fusion | flops 17181966336 | bytes 29360128 | tf_op jit(solution)/shard_map/dot_general | solution.py:38
  406.2 27.6 %fusion.17 = (f32[16,512]{1,0:T(8,128)S(1)}, f32[16,512,2048]{2,1,0:T(8,128)}) fusion(pred[2048]{0:T(1024)(128)(4,1)S(1)} %iota_compare_fusion, bf16[512,16,64]{0,2,1:T(8,128)(2,1)S(1)} %bitcast.23, bf16[2048,16,64]{0,2,1:T(8,128)(2,1)} %bitcast.24), kind=kOutput, calls=%fused_computation.30 | convolution fusion | flops 2197817344 | bytes 72386560 | tf_op jit(solution)/shard_map/sub | solution.py:47
  433.8 23.9 %convolution_convert_fusion.2 = bf16[2048,1024]{0,1:T(8,128)(2,1)} fusion(bf16[2048,4096]{1,0:T(8,128)(2,1)} %all-gather.3.cloned.1.call-done, bf16[4096,1024]{1,0:T(8,128)(2,1)} %param.16), kind=kOutput, calls=%fused_computation.15 | convolution fusion | flops 17181966336 | bytes 29360128 | tf_op jit(solution)/shard_map/dot_general | solution.py:39
  457.7 24.7 %fusion.13 = bf16[16,64,512]{2,1,0:T(8,128)(2,1)S(1)} fusion(bf16[2048,16,64]{0,2,1:T(8,128)(2,1)} %bitcast.25, f32[16,512,2048]{2,1,0:T(8,128)} %get-tuple-element.3, f32[16,512]{1,0:T(8,128)S(1)} %get-tuple-element.2), kind=kOutput, calls=%fused_computation.23 | convolution fusion | flops 2181562368 | bytes 72384512 | tf_op jit(solution)/shard_map/hqk,khd->qhd/dot_general | solution.py:49
  482.4 9.5 %convolution_convert_fusion = bf16[512,4096]{1,0:T(8,128)(2,1)} fusion(bf16[512,1024]{0,1:T(8,128)(2,1)S(1)} %bitcast.26, bf16[1024,4096]{1,0:T(8,128)(2,1)} %param.17), kind=kOutput, calls=%fused_computation.13 | convolution fusion | flops 4297064448 | bytes 13631488 | tf_op jit(solution)/shard_map/dot_general | solution.py:52
  491.9 0.0 reduce-scatter.2.cloned.1.call-update
  492.6 74.5 %reduce-scatter.2.cloned.1.call-done = bf16[128,4096]{1,0:T(8,128)(2,1)} async-done(((bf16[512,4096]{1,0:T(8,128)(2,1)}), bf16[128,4096]{1,0:T(8,128)(2,1)}) %reduce-scatter.2.cloned.1.call-update) | async-done | bytes 1048592 | tf_op jit(solution)/shard_map/reduce_scatter | solution.py:51
  567.0 2.5 select_convert_fusion
  (4 shorter events, 0.0 us)
Async XLA Ops:
  7.2 7.3 %copy-start = (f32[4096]{0:T(1024)S(1)}, f32[4096]{0:T(1024)}, u32[]{:S(2)}) copy-start(f32[4096]{0:T(1024)} %param.11) | copy-start | bytes 49156
  7.2 87.7 %all-gather.5.cloned.1.call-start = ((), (), s32[]{:S(2)}) async-start(), calls=%async_computation.2 | async-start | bytes 5242880 | tf_op jit(solution)/shard_map/all_gather | solution.py:34
  11.3 371.0 %all-gather.3.cloned.1.call-start = ((), (), s32[]{:S(2)}) async-start(), calls=%async_computation.1 | async-start | bytes 20971520 | tf_op jit(solution)/shard_map/all_gather | solution.py:37
  20.3 546.7 %reduce-scatter.2.cloned.1.call-start = ((), (), s32[]{:S(2)}) async-start(), calls=%async_computation.3 | async-start | bytes 5242880 | tf_op jit(solution)/shard_map/reduce_scatter | solution.py:51
Sparse Core Ops, SparseCore 0:
  11.4 83.4 all-gather.4
  97.1 285.2 all-gather.2
  492.0 74.9 reduce-scatter.1
where the time goes:
time: 576 us
  waiting for transfers between devices  426 us (74%)
  matrix products  119 us (21%)
  other arithmetic  15.5 us (3%)
  between operations  15.1 us (3%)
    all_gather x1, waiting for transfers between devices, shards(): segment = lax.all_gather(memory, 'tensor', axis=0, tiled=True)  278 us
    reduce_scatter x1, waiting for transfers between devices, shards(): lax.psum_scatter(jnp.dot(context, w_out, preferred_element_type=jnp.float...  74.5 us
    all_gather x1, waiting for transfers between devices, shards(): all_normed = lax.all_gather(normed, 'tensor', axis=0, tiled=True)  73.9 us
    sub x1, matrix products, shards(): weights = jax.nn.softmax(scores, axis=-1).astype(jnp.bfloat16)  27.6 us
    dot_general x1, matrix products, shards(): jnp.einsum('hqk,khd->qhd', weights, v_heads, preferred_element_type=jnp.f...  24.7 us
    dot_general x1, matrix products, shards(): jnp.dot(segment, w_key, preferred_element_type=jnp.float32)  23.9 us
    dot_general x1, matrix products, shards(): jnp.dot(segment, w_value, preferred_element_type=jnp.float32)  23.9 us
  transfers between devices with their start and end apart: 3, of which 3 were waited for; matrix products, arithmetic and copies ran while one was open for 3% of the time, Pallas kernels for 0%

commit v1 on v0

--- a/solution.py
+++ b/solution.py
@@ -31,7 +31,14 @@
     local_width = w_query.shape[1]
     local_heads = local_width // HEAD_DIM
     dec_rows = dec_hidden.shape[0]
-    all_normed = lax.all_gather(normed, "tensor", axis=0, tiled=True)
+    ways = lax.axis_size("tensor")
+    pieces = [normed]
+    for far in range(1, ways):
+        pieces.append(
+            lax.ppermute(pieces[far - 1], "tensor", [(d, (d - 1) % ways) for d in range(ways)])
+        )
+    line = jnp.concatenate(pieces, axis=0)
+    all_normed = jnp.roll(line, lax.axis_index("tensor") * normed.shape[0], axis=0)
     queries = jnp.dot(all_normed, w_query, preferred_element_type=jnp.float32).astype(jnp.bfloat16)
     q_heads = queries.reshape(DEC_LEN, local_heads, HEAD_DIM)
     segment = lax.all_gather(memory, "tensor", axis=0, tiled=True)

time: 576 us -> 559 us (0.970)
  waiting for transfers between devices: 426 us -> 397 us
  local copies, waits for them, and re-layouts: 0.73 us -> 8.21 us
  starting transfers between devices: 0.12 us -> 6.14 us
    ppermute x0 -> x3, waiting for transfers between devices: none -> 180 us  [shards(): lax.ppermute(pieces[far - 1], 'tensor', [(d, (d - 1) % ways) for d in ran...]
    all_gather x1, waiting for transfers between devices: 278 us -> 139 us  [shards(): segment = lax.all_gather(memory, 'tensor', axis=0, tiled=True)]
    all_gather x1 -> x0, waiting for transfers between devices: 73.9 us -> none  [shards(): all_normed = lax.all_gather(normed, 'tensor', axis=0, tiled=True)]
    unnamed x2 -> x10, local copies, waits for them, and re-layouts: 0.01 us -> 6.43 us
    ppermute x0 -> x3, starting transfers between devices: none -> 6.06 us  [shards(): lax.ppermute(pieces[far - 1], 'tensor', [(d, (d - 1) % ways) for d in ran...]
  transfers between devices with their start and end apart: 3 -> 5, of which waited for: 3 -> 5; matrix products, arithmetic and copies ran while one was open for 3% -> 3% of each run, Pallas kernels for 0% -> 0%
where the time goes in v1:
time: 559 us; the launch traced here: 558 us
  waiting for transfers between devices  397 us (71%)
  matrix products  119 us (21%)
  between operations  15.4 us (3%)
  other arithmetic  13.1 us (2%)
  local copies, waits for them, and re-layouts  8.21 us (1%)
  starting transfers between devices  6.14 us (1%)
    ppermute x3, waiting for transfers between devices, shards(): lax.ppermute(pieces[far - 1], 'tensor', [(d, (d - 1) % ways) for d in ran...  180 us
    all_gather x1, waiting for transfers between devices, shards(): segment = lax.all_gather(memory, 'tensor', axis=0, tiled=True)  139 us
    reduce_scatter x1, waiting for transfers between devices, shards(): lax.psum_scatter(jnp.dot(context, w_out, preferred_element_type=jnp.float...  78.3 us
    sub x1, matrix products, shards(): weights = jax.nn.softmax(scores, axis=-1).astype(jnp.bfloat16)  27.6 us
    dot_general x1, matrix products, shards(): jnp.einsum('hqk,khd->qhd', weights, v_heads, preferred_element_type=jnp.f...  24.7 us
    dot_general x1, matrix products, shards(): jnp.dot(segment, w_value, preferred_element_type=jnp.float32)  23.9 us
    dot_general x1, matrix products, shards(): jnp.dot(segment, w_key, preferred_element_type=jnp.float32)  23.9 us
  transfers between devices with their start and end apart: 5, of which 5 were waited for; matrix products, arithmetic and copies ran while one was open for 3% of the time, Pallas kernels for 0%

profile of v1, /device:TPU:0, one launch (start us, length us, event | category | flops | bytes accessed | tf_op | source)
XLA Modules:
  0.0 558.4 jit_solution(878557886000878071)
XLA Ops:
  7.2 0.0 copy-start
  7.2 0.0 all-gather.2.cloned.1.call-start
  7.2 3.2 fusion.7
  10.4 5.8 %fusion.9 = bf16[512,4096]{1,0:T(8,128)(2,1)} fusion(bf16[512,4096]{1,0:T(8,128)(2,1)} %param.10, f32[4096]{0:T(1024)} %param.11, f32[512]{0:T(512)S(1)} %add_rsqrt_fusion), kind=kLoop, calls=%fused_computation.12 | loop fusion | flops 8388608 | bytes 8407040 | tf_op jit(solution)/shard_map/convert_element_type | solution.py:14
  16.2 0.0 all-gather.2.cloned.1.call-update
  16.2 0.0 reduce-scatter.2.cloned.1.call-start
  16.2 0.3 fusion.12
  16.5 1.4 constant_dynamic-update-slice_fusion.7
  17.9 5.1 collective-permute-start
  23.0 41.0 %collective-permute-done = bf16[128,4096]{1,0:T(8,128)(2,1)S(1)} collective-permute-done((bf16[128,4096]{1,0:T(8,128)(2,1)S(1)}, bf16[128,4096]{1,0:T(8,128)(2,1)S(1)}, u32[]{:S(2)}, u32[]{:S(2)}) %collective-permute-start) | collective-permute-done | bytes 1048608 | tf_op jit(solution)/shard_map/ppermute | solution.py:38
  64.0 1.0 collective-permute-start.1
  65.6 71.6 %collective-permute-done.1 = bf16[128,4096]{1,0:T(8,128)(2,1)S(1)} collective-permute-done((bf16[128,4096]{1,0:T(8,128)(2,1)S(1)}, bf16[128,4096]{1,0:T(8,128)(2,1)S(1)}, u32[]{:S(2)}, u32[]{:S(2)}) %collective-permute-start.1) | collective-permute-done | bytes 1048608 | tf_op jit(solution)/shard_map/ppermute | solution.py:38
  137.2 0.0 collective-permute-start.2
  137.3 1.1 constant_dynamic-update-slice_fusion.6
  138.4 1.1 constant_dynamic-update-slice_fusion.5
  139.4 67.0 %collective-permute-done.2 = bf16[128,4096]{1,0:T(8,128)(2,1)S(1)} collective-permute-done((bf16[128,4096]{1,0:T(8,128)(2,1)S(1)}, bf16[128,4096]{1,0:T(8,128)(2,1)S(1)}, u32[]{:S(2)}, u32[]{:S(2)}) %collective-permute-start.2) | collective-permute-done | bytes 1048608 | tf_op jit(solution)/shard_map/ppermute | solution.py:38
  206.4 1.1 constant_dynamic-update-slice_fusion.4
  207.5 1.0 constant_dynamic-update-slice_fusion.3
  208.5 1.1 constant_dynamic-update-slice_fusion.2
  209.6 1.1 constant_dynamic-update-slice_fusion.1
  210.7 1.0 constant_dynamic-update-slice_fusion
  211.7 9.2 %fusion.15 = bf16[512,1024]{1,0:T(8,128)(2,1)S(1)} fusion(bf16[4096,1024]{1,0:T(8,128)(2,1)} %param.14, bf16[1024,4096]{1,0:T(8,128)(2,1)} %constant_dynamic-update-slice_fusion, s32[]{:T(128)S(6)} %select_n.22), kind=kOutput, calls=%fused_computation.24 | convolution fusion | flops 4295491584 | bytes 13631492 | tf_op jit(solution)/shard_map/dot_general | solution.py:42
  220.9 0.7 copy.13
  221.6 139.0 %all-gather.2.cloned.1.call-done = bf16[2048,4096]{1,0:T(8,128)(2,1)} async-done(((bf16[512,4096]{1,0:T(8,128)(2,1)}), bf16[2048,4096]{1,0:T(8,128)(2,1)}) %all-gather.2.cloned.1.call-update) | async-done | bytes 16777232 | tf_op jit(solution)/shard_map/all_gather | solution.py:44
  360.6 23.9 %convolution_convert_fusion.1 = bf16[2048,1024]{0,1:T(8,128)(2,1)} fusion(bf16[2048,4096]{1,0:T(8,128)(2,1)} %all-gather.2.cloned.1.call-done, bf16[4096,1024]{1,0:T(8,128)(2,1)} %param.15), kind=kOutput, calls=%fused_computation.16 | convolution fusion | flops 17181966336 | bytes 29360128 | tf_op jit(solution)/shard_map/dot_general | solution.py:45
  384.5 27.6 %fusion.24 = (f32[16,512]{1,0:T(8,128)S(1)}, f32[16,512,2048]{2,1,0:T(8,128)}) fusion(pred[2048]{0:T(1024)(128)(4,1)S(1)} %iota_compare_fusion, bf16[512,16,64]{0,2,1:T(8,128)(2,1)S(1)} %bitcast.22, bf16[2048,16,64]{0,2,1:T(8,128)(2,1)} %bitcast.23), kind=kOutput, calls=%fused_computation.41 | convolution fusion | flops 2197817344 | bytes 72386560 | tf_op jit(solution)/shard_map/sub | solution.py:54
  412.0 23.9 %convolution_convert_fusion.2 = bf16[2048,1024]{0,1:T(8,128)(2,1)} fusion(bf16[2048,4096]{1,0:T(8,128)(2,1)} %all-gather.2.cloned.1.call-done, bf16[4096,1024]{1,0:T(8,128)(2,1)} %param.16), kind=kOutput, calls=%fused_computation.17 | convolution fusion | flops 17181966336 | bytes 29360128 | tf_op jit(solution)/shard_map/dot_general | solution.py:46
  435.9 24.7 %fusion.18 = bf16[16,64,512]{2,1,0:T(8,128)(2,1)S(1)} fusion(bf16[2048,16,64]{0,2,1:T(8,128)(2,1)} %bitcast.24, f32[16,512,2048]{2,1,0:T(8,128)} %get-tuple-element.5, f32[16,512]{1,0:T(8,128)S(1)} %get-tuple-element.4), kind=kOutput, calls=%fused_computation.25 | convolution fusion | flops 2181562368 | bytes 72384512 | tf_op jit(solution)/shard_map/hqk,khd->qhd/dot_general | solution.py:56
  460.6 9.5 %convolution_convert_fusion = bf16[512,4096]{1,0:T(8,128)(2,1)} fusion(bf16[512,1024]{0,1:T(8,128)(2,1)S(1)} %bitcast.25, bf16[1024,4096]{1,0:T(8,128)(2,1)} %param.17), kind=kOutput, calls=%fused_computation.13 | convolution fusion | flops 4297064448 | bytes 13631488 | tf_op jit(solution)/shard_map/dot_general | solution.py:59
  470.1 0.0 reduce-scatter.2.cloned.1.call-update
  470.8 78.3 %reduce-scatter.2.cloned.1.call-done = bf16[128,4096]{1,0:T(8,128)(2,1)} async-done(((bf16[512,4096]{1,0:T(8,128)(2,1)}), bf16[128,4096]{1,0:T(8,128)(2,1)}) %reduce-scatter.2.cloned.1.call-update) | async-done | bytes 1048592 | tf_op jit(solution)/shard_map/reduce_scatter | solution.py:58
  549.1 2.5 select_convert_fusion
  (7 shorter events, 0.0 us)
Async XLA Ops:
  7.2 9.1 %copy-start = (bf16[128,4096]{1,0:T(8,128)(2,1)S(1)}, bf16[128,4096]{1,0:T(8,128)(2,1)}, u32[]{:S(2)}) copy-start(bf16[128,4096]{1,0:T(8,128)(2,1)} %param.12) | copy-start | bytes 3145732
  7.2 9.4 %copy-start.1 = (f32[4096]{0:T(1024)S(1)}, f32[4096]{0:T(1024)}, u32[]{:S(2)}) copy-start(f32[4096]{0:T(1024)} %param.13) | copy-start | bytes 49156
  7.2 353.4 %all-gather.2.cloned.1.call-start = ((), (), s32[]{:S(2)}) async-start(), calls=%async_computation.1 | async-start | bytes 20971520 | tf_op jit(solution)/shard_map/all_gather | solution.py:44
  16.2 532.9 %reduce-scatter.2.cloned.1.call-start = ((), (), s32[]{:S(2)}) async-start(), calls=%async_computation.2 | async-start | bytes 5242880 | tf_op jit(solution)/shard_map/reduce_scatter | solution.py:58
  17.9 46.1 %collective-permute-start = (bf16[128,4096]{1,0:T(8,128)(2,1)S(1)}, bf16[128,4096]{1,0:T(8,128)(2,1)S(1)}, u32[]{:S(2)}, u32[]{:S(2)}) collective-permute-start(bf16[128,4096]{1,0:T(8,128)(2,1)S(1)} %get-tuple-element.3), channel_id=1, source_target_pairs={{0,3},{1,0},{2,1},{3,2},{4,7},{5,4},{6,5},{7,6},{8,11},{9,8},{10,9... | collective-permute-start | bytes 3145736 | tf_op jit(solution)/shard_map/ppermute | solution.py:38
  64.0 73.2 %collective-permute-start.1 = (bf16[128,4096]{1,0:T(8,128)(2,1)S(1)}, bf16[128,4096]{1,0:T(8,128)(2,1)S(1)}, u32[]{:S(2)}, u32[]{:S(2)}) collective-permute-start(bf16[128,4096]{1,0:T(8,128)(2,1)S(1)} %collective-permute-done), channel_id=1, source_target_pairs={{0,3},{1,0},{2,1},{3,2},{4,7},{5,4},{6,5},{7,6},{8,11},{9,8},{10,9... | collective-permute-start | bytes 3145736 | tf_op jit(solution)/shard_map/ppermute | solution.py:38
  137.2 69.2 %collective-permute-start.2 = (bf16[128,4096]{1,0:T(8,128)(2,1)S(1)}, bf16[128,4096]{1,0:T(8,128)(2,1)S(1)}, u32[]{:S(2)}, u32[]{:S(2)}) collective-permute-start(bf16[128,4096]{1,0:T(8,128)(2,1)S(1)} %collective-permute-done.1), channel_id=1, source_target_pairs={{0,3},{1,0},{2,1},{3,2},{4,7},{5,4},{6,5},{7,6},{8,11},{9,8},{10,9... | collective-permute-start | bytes 3145736 | tf_op jit(solution)/shard_map/ppermute | solution.py:38
Sparse Core Ops, SparseCore 0:
  16.3 344.2 all-gather.1
  470.3 78.8 reduce-scatter.1
